TPU v7x, 256 devices: a whole 4x4x8 slice. The times are simulated.
256 devices in a mesh: seq: 8 (over y, core), tensor: 32 (over z, x).
Axes of the slice: x: 4, y: 4, z: 8, core: 2. Of those that a mesh axis runs over, the one named last changes fastest.
Arguments:
- tokens: bfloat16 [4096, 3584], P('seq', 'tensor'), may hold values from -6 to 6
- w_zx: bfloat16 [2, 3584, 4096], P(None, None, 'tensor'), may hold values from -0.09375 to 0.09375
- w_bc: bfloat16 [3584, 128], replicated, may hold values from -0.09375 to 0.09375
- w_dt: bfloat16 [3584, 64], P(None, 'tensor'), may hold values from -0.09375 to 0.09375
- dt_bias: float32 [64], P('tensor'), may hold values from -2 to 0.5
- a_rate: float32 [64], P('tensor'), may hold values from 0.00012207031 to 0.05
- d_skip: float32 [64], P('tensor'), may hold values from 0.3 to 1.5
- conv_x: float32 [4, 4096], P(None, 'tensor'), may hold values from -3 to 3
- conv_bc: float32 [4, 128], replicated, may hold values from -3 to 3
- norm_gain: float32 [4096], P('tensor'), may hold values from 0.25 to 1.75
- w_out: bfloat16 [4096, 3584], P('tensor'), may hold values from -0.09375 to 0.09375
- segments: int32 [4096], P('seq'), may hold values from 0 to 5, never falling along the last dimension, each value on 1 to 2048 neighbouring positions
Outputs:
- mixed: bfloat16 [4096, 3584], P(('seq', 'tensor'))
Inputs may be any that keep to these rules, and one draw needn't show every extreme that they name: `segments`: prompt ids never fall along the tokens, so each prompt's tokens are contiguous.
All inputs are finite; a program needn't handle non-finite values.
Results may differ from a plain program's by a relative error of at most 0.02.
Values may be sent and summed in bfloat16 or wider, within the bound.
A program may use at most 64 MiB of HBM per device.

v0:
```python
import jax
import jax.numpy as jnp
from jax import lax
from jax.sharding import PartitionSpec as P

BLOCK = 256
HIGHEST_PREC = lax.Precision.HIGHEST
NORM_EPS = 1e-05


def from_behind(block, axis, distance):
    devices = range(lax.axis_size(axis))
    route = [(i - distance, i) for i in devices if i - distance in devices]
    return lax.ppermute(block, axis, route)


def entering(array, axis, join, neutral):
    place = lax.axis_index(axis)
    gathered = jax.tree.map(
        lambda a, kind: lax.all_gather(a.astype(kind), axis),
        array,
        jax.tree.map(lambda a: jnp.bfloat16 if a.dtype == jnp.float32 else a.dtype, array),
    )
    state = jax.tree.map(lambda a, e: jnp.zeros_like(a) + jnp.asarray(e, a.dtype), array, neutral)

    def one(turn, state):
        return join(
            state,
            jax.tree.map(
                lambda a, own: lax.dynamic_index_in_dim(a, turn, 0, False).astype(own.dtype),
                gathered,
                array,
            ),
        )

    return lax.fori_loop(0, place, one, state)


def conv_tail(extended, seg_ext, taps, tok_rows):
    conv_len = taps.shape[0]
    seg_now = seg_ext[conv_len - 1 :]
    conv_sum = taps[conv_len - 1] * extended[conv_len - 1 :]
    for offset in range(1, conv_len):
        earlier = extended[conv_len - 1 - offset : conv_len - 1 - offset + tok_rows]
        seg_then = seg_ext[conv_len - 1 - offset : conv_len - 1 - offset + tok_rows]
        conv_sum = conv_sum + taps[conv_len - 1 - offset] * jnp.where(
            (seg_then == seg_now)[:, None], earlier, 0.0
        )
    return jax.nn.silu(conv_sum)


def ssd_block(carry, block):
    state, last_seg = carry
    inner_x, step_size, logdec, bmat, cmat, seg_ids = block
    cum_decay = jnp.cumsum(logdec, axis=0)
    position = jnp.arange(seg_ids.shape[0])
    visible = (seg_ids[:, None] == seg_ids[None, :]) & (position[:, None] >= position[None, :])
    gap_decay = jnp.where(
        visible[:, :, None], cum_decay[:, None, :] - cum_decay[None, :, :], -jnp.inf
    )
    scores = jnp.dot(cmat, bmat.T, precision=HIGHEST_PREC)
    weights = jnp.exp(gap_decay) * scores[:, :, None] * step_size[None, :, :]
    block_out = jnp.einsum("tsh,shp->thp", weights, inner_x, precision=HIGHEST_PREC)
    enter = jnp.where((seg_ids == last_seg)[:, None], jnp.exp(cum_decay), 0.0)
    block_out = block_out + enter[:, :, None] * jnp.einsum(
        "tn,hpn->thp", cmat, state, precision=HIGHEST_PREC
    )
    tail_weight = (
        jnp.where(
            (seg_ids == seg_ids[-1])[:, None], jnp.exp(cum_decay[-1][None, :] - cum_decay), 0.0
        )
        * step_size
    )
    carry_keep = jnp.where(seg_ids[-1] == last_seg, jnp.exp(cum_decay[-1]), 0.0)
    new_state = carry_keep[:, None, None] * state + jnp.einsum(
        "sh,shp,sn->hpn", tail_weight, inner_x, bmat, precision=HIGHEST_PREC
    )
    return ((new_state, seg_ids[-1]), block_out)


def link_states(earlier, later):
    gain_a, state_a, first_a, last_a = earlier
    gain_b, state_b, first_b, last_b = later
    joined = (first_b == last_a) | (last_a < 0.0) | (first_b < 0.0)
    passing = jnp.where(joined, gain_b, 0.0)
    merged_gain = gain_a * passing
    merged_state = passing[:, None, None] * state_a + state_b
    merged_first = jnp.where(first_a < 0.0, first_b, first_a)
    merged_last = jnp.where(last_b < 0.0, last_a, last_b)
    return (merged_gain, merged_state, merged_first, merged_last)


def local(
    tokens, w_zx, w_bc, w_dt, dt_bias, a_rate, d_skip, conv_x, conv_bc, norm_gain, w_out, segments
):
    tok_rows = tokens.shape[0]
    inner_w = w_zx.shape[2]
    heads = dt_bias.shape[0]
    head_size = inner_w // heads
    state_w = w_bc.shape[1] // 2
    rim_len = conv_x.shape[0] - 1
    piece = lax.all_gather(tokens, "tensor", axis=1, tiled=True)
    gate_rows = w_zx[0]
    inner_rows = w_zx[1]
    gate_sum = jnp.dot(piece, gate_rows, preferred_element_type=jnp.float32)
    inner_sum = jnp.dot(piece, inner_rows, preferred_element_type=jnp.float32)
    bc_sum = jnp.dot(piece, w_bc, preferred_element_type=jnp.float32)
    dt_raw = jnp.dot(piece, w_dt, preferred_element_type=jnp.float32)
    gate_proj = gate_sum.astype(jnp.bfloat16)
    inner_proj = inner_sum.astype(jnp.bfloat16)
    bc_proj = bc_sum.astype(jnp.bfloat16)
    rim_inner, rim_bc, rim_seg = from_behind(
        (
            inner_proj[tok_rows - rim_len :],
            bc_proj[tok_rows - rim_len :],
            segments[tok_rows - rim_len :].astype(jnp.bfloat16),
        ),
        "seq",
        1,
    )
    seg_ext = jnp.concatenate([rim_seg.astype(jnp.int32), segments], 0)
    conv_inner = conv_tail(
        jnp.concatenate([rim_inner.astype(jnp.float32), inner_proj.astype(jnp.float32)], 0),
        seg_ext,
        conv_x,
        tok_rows,
    )
    conv_state = conv_tail(
        jnp.concatenate([rim_bc.astype(jnp.float32), bc_proj.astype(jnp.float32)], 0),
        seg_ext,
        conv_bc,
        tok_rows,
    )
    bmat = conv_state[:, :state_w]
    cmat = conv_state[:, state_w:]
    step_size = jax.nn.softplus(dt_raw + dt_bias)
    logdec = -a_rate * step_size
    inner_heads = conv_inner.reshape(tok_rows, heads, head_size)
    nblocks = tok_rows // BLOCK
    blocks = (
        inner_heads.reshape(nblocks, BLOCK, heads, head_size),
        step_size.reshape(nblocks, BLOCK, heads),
        logdec.reshape(nblocks, BLOCK, heads),
        bmat.reshape(nblocks, BLOCK, state_w),
        cmat.reshape(nblocks, BLOCK, state_w),
        segments.reshape(nblocks, BLOCK),
    )
    start_carry = (jnp.zeros((heads, head_size, state_w), jnp.float32), jnp.array(-1, jnp.int32))
    (local_state, _), block_outs = lax.scan(ssd_block, start_carry, blocks)
    cum_device = jnp.cumsum(logdec, axis=0)
    device_gain = jnp.where(segments[0] == segments[-1], jnp.exp(cum_device[-1]), 0.0)
    seg_float = segments.astype(jnp.float32)
    element = (device_gain, local_state, seg_float[:1], seg_float[-1:])
    identity = (
        jnp.ones((heads,), jnp.float32),
        jnp.zeros_like(local_state),
        jnp.full((1,), -1.0, jnp.float32),
        jnp.full((1,), -1.0, jnp.float32),
    )
    incoming = entering(element, "seq", link_states, identity)
    state_in = incoming[1]
    last_in = incoming[3]
    enter = jnp.where((seg_float == last_in[0])[:, None], jnp.exp(cum_device), 0.0)
    ssd_out = block_outs.reshape(tok_rows, heads, head_size)
    ssd_out = ssd_out + enter[:, :, None] * jnp.einsum(
        "tn,hpn->thp", cmat, state_in, precision=HIGHEST_PREC
    )
    ssd_out = ssd_out + d_skip[None, :, None] * inner_heads
    gated = ssd_out.reshape(tok_rows, inner_w) * jax.nn.silu(gate_proj.astype(jnp.float32))
    local_squares = jnp.sum(gated * gated, axis=1)
    total_squares = lax.psum(local_squares, "tensor")
    scale = lax.rsqrt(total_squares / (inner_w * lax.axis_size("tensor")) + NORM_EPS)
    normed = (gated * scale[:, None] * norm_gain).astype(jnp.bfloat16)
    return lax.psum_scatter(
        jnp.dot(normed, w_out, preferred_element_type=jnp.float32).astype(jnp.bfloat16),
        "tensor",
        scatter_dimension=0,
        tiled=True,
    )


def solution(mesh):
    in_specs = (
        P("seq", "tensor"),
        P(None, None, "tensor"),
        P(),
        P(None, "tensor"),
        P("tensor"),
        P("tensor"),
        P("tensor"),
        P(None, "tensor"),
        P(),
        P("tensor"),
        P("tensor", None),
        P("seq"),
    )
    out_specs = P(("seq", "tensor"), None)
    return jax.shard_map(local, mesh=mesh, in_specs=in_specs, out_specs=out_specs, check_vma=False)
```

profile of v0, /device:TPU:8, one launch (start us, length us, event | category | flops | bytes accessed | tf_op | source)
XLA Modules:
  0.0 471.1 jit_solution(9409055045789982205)
XLA Ops:
  6.5 0.7 all-gather.6.cloned.1.call-update
  7.3 0.8 convert_convert_fusion
  8.2 1.3 dynamic-slice
  9.4 0.6 fusion.82
  10.0 1.4 dynamic-update-slice
  11.4 1.3 dynamic-update-slice.1
  12.7 1.9 collective-permute-start
  14.6 12.0 %all-reduce.2 = (bf16[8]{0:T(256)(128)(2,1)S(1)}, bf16[8]{0:T(256)(128)(2,1)S(1)}) all-reduce(bf16[8]{0:T(256)(128)(2,1)S(1)} %dynamic-update-slice, bf16[8]{0:T(256)(128)(2,1)S(1)} %dynamic-update-slice.1), channel_id=2, replica_groups=mesh['seq'=8,'tensor'=32] {'seq'}, use_global_device_ids=true, to_apply=%add | all-reduce | flops 16 | bytes 64
  26.6 0.7 reshape.139
  27.3 0.7 neg.20
  28.0 1.4 fusion.81
  30.7 0.8 slice_bitcast_fusion.8
  31.6 0.8 slice_bitcast_fusion.4
  32.4 0.8 pad_add_fusion
  33.2 0.8 slice_compare_fusion.2
  33.9 59.5 %all-gather.6.cloned.1.call-done = bf16[512,3584]{0,1:T(8,128)(2,1)} async-done(((bf16[512,112]{0,1:T(8,128)(2,1)}), bf16[512,3584]{0,1:T(8,128)(2,1)}) %all-gather.6.cloned.1.call-update) | async-done | bytes 3670032 | tf_op jit(solution)/shard_map/all_gather | solution.py:102
  93.4 2.7 broadcast_multiply_fusion
  96.3 3.6 fusion.83
  99.9 1.9 collective-permute-start.1
  101.8 1.1 fusion.84
  103.0 3.5 collective-permute-start.2
  106.6 0.6 reduce-window.16
  107.8 8.4 %all-gather.3 = bf16[8,1,2]{2,1,0:T(2,128)(2,1)S(1)} all-gather(bf16[1,1,2]{2,1,0:T(2,128)(2,1)S(1)} %bitcast.197), channel_id=1, replica_groups=mesh['seq'=8,'tensor'=32] {'seq'}, dimensions={0}, use_global_device_ids=true | all-gather | bytes 36 | tf_op jit(solution)/shard_map/all_gather | solution.py:20
  116.3 0.3 divide_multiply_fusion.1
  116.6 0.3 reshape.172
  117.3 0.3 divide_multiply_fusion
  118.0 16.2 %while.31 = (s32[]{:T(128)}, f32[2,64,64]{2,1,0:T(8,128)S(1)}, s32[]{:T(128)}, f32[2,256,2,64]{1,0,3,2:T(2,128)S(1)}, s32[2,256]{1,0:T(2,128)S(1)}, /*index=5*/f...) while((s32[]{:T(128)}, f32[2,64,64]{2,1,0:T(8,128)S(1)}, ...), condition=%wide.region_3.4_spmd.clone, body=%wide.region_0.3_spmd.clone.sunk | while | flops 202246672 | bytes 2326889 | solution.py:149
  118.0 0.6 reduce-window.26
  119.2 0.6 dynamic-slice.4
  119.8 0.6 broadcast_compare_fusion.3
  122.0 0.4 fusion.112
  122.6 0.8 fusion.114
  123.6 1.9 dynamic_update_slice.6
  126.1 0.6 reduce-window.26
  127.3 0.6 dynamic-slice.4
  127.9 0.6 broadcast_compare_fusion.3
  130.1 0.4 fusion.112
  130.7 0.8 fusion.114
  131.6 1.9 dynamic_update_slice.6
  134.4 11.6 %all-gather.1 = bf16[16,64,64]{2,1,0:T(8,128)(2,1)S(1)} all-gather(bf16[2,64,64]{2,1,0:T(8,128)(2,1)S(1)} %convert_element_type.85), channel_id=3, replica_groups=mesh['seq'=8,'tensor'=32] {'seq'}, dimensions={0}, use_global_device_ids=true | all-gather | bytes 147456 | tf_op jit(solution)/shard_map/all_gather | solution.py:20
  146.0 6.9 %while.30 = (s32[]{:T(128)}, f32[2,64,64]{2,1,0:T(8,128)S(1)}, f32[1]{0:T(128)}, s32[]{:T(128)}, bf16[8,1]{0,1:T(2,128)(2,1)S(1)}, /*index=5*/bf16[8,2]{0,1:T(2,...) while((s32[]{:T(128)}, f32[2,64,64]{2,1,0:T(8,128)S(1)}, ...), condition=%wide.region_7.8_spmd, body=%wide.region_6.7_spmd.sunk | while | flops 24592 | bytes 82183 | solution.py:36
  146.0 0.6 constant_dynamic-slice_fusion.7
  149.5 0.6 constant_dynamic-slice_fusion.7
  152.9 0.5 fusion.38
  153.6 3.5 multiply_reduce_fusion
  157.1 71.9 %psum.7 = f32[512]{0:T(512)S(1)} all-reduce(f32[512]{0:T(512)S(1)} %get-tuple-element.290), channel_id=1, replica_groups=mesh['seq'=8,'tensor'=32] {'tensor'}, use_global_device_ids=true, to_apply=%region_9.10 | all-reduce | flops 512 | bytes 4096 | tf_op jit(solution)/shard_map/psum | solution.py:171
  229.1 3.0 convolution_convert_fusion
  232.1 232.2 %reduce-scatter.2.cloned.1.call-done = bf16[16,3584]{1,0:T(8,128)(2,1)} async-done(((bf16[512,3584]{1,0:T(8,128)(2,1)}), bf16[16,3584]{1,0:T(8,128)(2,1)}) %reduce-scatter.2.cloned.1.call-update) | async-done | bytes 114704 | tf_op jit(solution)/shard_map/reduce_scatter | solution.py:174
  (93 shorter events, 6.4 us)
Async XLA Ops:
  6.5 222.5 %copy-start = (bf16[128,3584]{1,0:T(8,128)(2,1)S(1)}, bf16[128,3584]{1,0:T(8,128)(2,1)}, u32[]{:S(2)}) copy-start(bf16[128,3584]{1,0:T(8,128)(2,1)} %param.26) | copy-start | bytes 2752516
  6.5 86.9 %all-gather.6.cloned.1.call-start = ((), (), s32[]{:S(2)}) async-start(), calls=%async_computation.1 | async-start | bytes 3784704 | tf_op jit(solution)/shard_map/all_gather | solution.py:102
  7.3 457.0 %reduce-scatter.2.cloned.1.call-start = ((), (), s32[]{:S(2)}) async-start(), calls=%async_computation.2 | async-start | bytes 3784704 | tf_op jit(solution)/shard_map/reduce_scatter | solution.py:174
  12.7 19.7 %collective-permute-start = (bf16[3]{0:T(256)(128)(2,1)S(1)}, bf16[3]{0:T(256)(128)(2,1)S(1)}, u32[]{:S(2)}, u32[]{:S(2)}) collective-permute-start(bf16[3]{0:T(256)(128)(2,1)S(1)} %slice.118), channel_id=1, source_target_pairs={{0,32},{32,64},{64,96},{96,128},{128,160},{160,192},{192,224},{1,3... | collective-permute-start | bytes 26 | tf_op jit(solution)/shard_map/ppermute | solution.py:14
  96.1 5.7 %copy-start.2 = (bf16[3584,128]{1,0:T(8,128)(2,1)S(1)}, bf16[3584,128]{1,0:T(8,128)(2,1)}, u32[]{:S(2)}) copy-start(bf16[3584,128]{1,0:T(8,128)(2,1)} %param.18) | copy-start | bytes 2752516
  96.2 5.6 %copy-start.1 = (bf16[512,3584]{0,1:T(8,128)(2,1)S(1)}, bf16[512,3584]{0,1:T(8,128)(2,1)}, u32[]{:S(2)}) copy-start(bf16[512,3584]{0,1:T(8,128)(2,1)} %all-gather.6.cloned.1.call-done) | copy-start | bytes 11010052
  99.9 16.4 %collective-permute-start.1 = (bf16[3,128]{1,0:T(4,128)(2,1)S(1)}, bf16[3,128]{1,0:T(4,128)(2,1)S(1)}, u32[]{:S(2)}, u32[]{:S(2)}) collective-permute-start(bf16[3,128]{1,0:T(4,128)(2,1)S(1)} %slice.152), channel_id=1, source_target_pairs={{0,32},{32,64},{64,96},{96,128},{128,160},{160,192},{192,224},{1,3... | collective-permute-start | bytes 2312 | tf_op jit(solution)/shard_map/ppermute | solution.py:14
  103.0 14.3 %collective-permute-start.2 = (bf16[3,128]{1,0:T(4,128)(2,1)S(1)}, bf16[3,128]{1,0:T(4,128)(2,1)S(1)}, u32[]{:S(2)}, u32[]{:S(2)}) collective-permute-start(bf16[3,128]{1,0:T(4,128)(2,1)S(1)} %slice.157), channel_id=1, source_target_pairs={{0,32},{32,64},{64,96},{96,128},{128,160},{160,192},{192,224},{1,3... | collective-permute-start | bytes 2312 | tf_op jit(solution)/shard_map/ppermute | solution.py:14
  117.9 35.0 %copy-start.3 = (s32[512]{0:T(512)S(1)}, s32[512]{0:T(512)}, u32[]{:S(2)}) copy-start(s32[512]{0:T(512)} %param.27) | copy-start | bytes 6148
  117.9 35.0 %copy-start.5 = (f32[2]{0:T(128)S(1)}, f32[2]{0:T(128)}, u32[]{:S(2)}) copy-start(f32[2]{0:T(128)} %param.22) | copy-start | bytes 28
  153.5 75.6 %copy-start.4 = (f32[128]{0:T(128)S(1)}, f32[128]{0:T(128)}, u32[]{:S(2)}) copy-start(f32[128]{0:T(128)} %param.25) | copy-start | bytes 1540
Sparse Core Ops, SparseCore 0:
  9.9 83.4 all-gather.5
  232.2 232.0 reduce-scatter.1
where the time goes:
time: 472 us; the launch traced here: 471 us
  waiting for transfers between devices  292 us (62%)
  blocking collectives  104 us (22%)
  local copies, waits for them, and re-layouts  18.2 us (4%)
  matrix products  17.9 us (4%)
  between operations  15 us (3%)
  other arithmetic  8.35 us (2%)
  loops' own time  7.88 us (2%)
  starting transfers between devices  7.37 us (2%)
    reduce_scatter x1, waiting for transfers between devices, local(): lax.psum_scatter(jnp.dot(normed, w_out, preferred_element_type=jnp.float3...  232 us
    psum x1, blocking collectives, local(): total_squares = lax.psum(local_squares, 'tensor')  71.9 us
    all_gather x1, waiting for transfers between devices, local(): piece = lax.all_gather(tokens, 'tensor', axis=1, tiled=True)  59.5 us
    all_gather x2, blocking collectives, entering(): lax.all_gather(a.astype(kind), axis)  20 us
    unnamed x1, blocking collectives  12 us
  transfers between devices with their start and end apart: 5, of which 2 were waited for; matrix products, arithmetic and copies ran while one was open for 3% of the time, Pallas kernels for 0%

commit v1 on v0

--- a/solution.py
+++ b/solution.py
@@ -168,7 +168,8 @@
     ssd_out = ssd_out + d_skip[None, :, None] * inner_heads
     gated = ssd_out.reshape(tok_rows, inner_w) * jax.nn.silu(gate_proj.astype(jnp.float32))
     local_squares = jnp.sum(gated * gated, axis=1)
-    total_squares = lax.psum(local_squares, "tensor")
+    parts = lax.all_gather(local_squares, "tensor", axis=0, tiled=False)
+    total_squares = parts.sum(axis=0)
     scale = lax.rsqrt(total_squares / (inner_w * lax.axis_size("tensor")) + NORM_EPS)
     normed = (gated * scale[:, None] * norm_gain).astype(jnp.bfloat16)
     return lax.psum_scatter(

time: 472 us -> 449 us (0.951)
  blocking collectives: 104 us -> 79.3 us
    psum x1 -> x0, blocking collectives: 71.9 us -> none  [local(): total_squares = lax.psum(local_squares, 'tensor')]
    all_gather x0 -> x1, blocking collectives: none -> 47.3 us  [local(): parts = lax.all_gather(local_squares, 'tensor', axis=0, tiled=False)]
where the time goes in v1:
time: 449 us; the launch traced here: 448 us
  waiting for transfers between devices  294 us (65%)
  blocking collectives  79.3 us (18%)
  local copies, waits for them, and re-layouts  18.2 us (4%)
  matrix products  17.9 us (4%)
  between operations  15 us (3%)
  other arithmetic  8.42 us (2%)
  loops' own time  7.88 us (2%)
  starting transfers between devices  7.37 us (2%)
    reduce_scatter x1, waiting for transfers between devices, local(): lax.psum_scatter(jnp.dot(normed, w_out, preferred_element_type=jnp.float3...  234 us
    all_gather x1, waiting for transfers between devices, local(): piece = lax.all_gather(tokens, 'tensor', axis=1, tiled=True)  59.5 us
    all_gather x1, blocking collectives, local(): parts = lax.all_gather(local_squares, 'tensor', axis=0, tiled=False)  47.3 us
    all_gather x2, blocking collectives, entering(): lax.all_gather(a.astype(kind), axis)  20 us
    unnamed x1, blocking collectives  12 us
  transfers between devices with their start and end apart: 5, of which 2 were waited for; matrix products, arithmetic and copies ran while one was open for 3% of the time, Pallas kernels for 0%

profile of v1, /device:TPU:8, one launch (start us, length us, event | category | flops | bytes accessed | tf_op | source)
XLA Modules:
  0.0 448.0 jit_solution(17487057363028681952)
XLA Ops:
  6.5 0.7 all-gather.8.cloned.1.call-update
  7.3 0.8 convert_convert_fusion
  8.2 1.3 dynamic-slice
  9.4 0.6 fusion.82
  10.0 1.4 dynamic-update-slice
  11.4 1.3 dynamic-update-slice.1
  12.7 1.9 collective-permute-start
  14.6 12.0 %all-reduce.2 = (bf16[8]{0:T(256)(128)(2,1)S(1)}, bf16[8]{0:T(256)(128)(2,1)S(1)}) all-reduce(bf16[8]{0:T(256)(128)(2,1)S(1)} %dynamic-update-slice, bf16[8]{0:T(256)(128)(2,1)S(1)} %dynamic-update-slice.1), channel_id=2, replica_groups=mesh['seq'=8,'tensor'=32] {'seq'}, use_global_device_ids=true, to_apply=%add | all-reduce | flops 16 | bytes 64
  26.6 0.7 reshape.143
  27.3 0.7 neg.20
  28.0 1.4 fusion.81
  30.7 0.8 slice_bitcast_fusion.8
  31.6 0.8 slice_bitcast_fusion.4
  32.4 0.8 pad_add_fusion
  33.2 0.8 slice_compare_fusion.2
  33.9 59.5 %all-gather.8.cloned.1.call-done = bf16[512,3584]{0,1:T(8,128)(2,1)} async-done(((bf16[512,112]{0,1:T(8,128)(2,1)}), bf16[512,3584]{0,1:T(8,128)(2,1)}) %all-gather.8.cloned.1.call-update) | async-done | bytes 3670032 | tf_op jit(solution)/shard_map/all_gather | solution.py:102
  93.4 2.7 broadcast_multiply_fusion
  96.3 3.6 fusion.83
  99.9 1.9 collective-permute-start.1
  101.8 1.1 fusion.84
  103.0 3.5 collective-permute-start.2
  106.6 0.6 reduce-window.16
  107.8 8.4 %all-gather.4 = bf16[8,1,2]{2,1,0:T(2,128)(2,1)S(1)} all-gather(bf16[1,1,2]{2,1,0:T(2,128)(2,1)S(1)} %bitcast.199), channel_id=1, replica_groups=mesh['seq'=8,'tensor'=32] {'seq'}, dimensions={0}, use_global_device_ids=true | all-gather | bytes 36 | tf_op jit(solution)/shard_map/all_gather | solution.py:20
  116.3 0.3 divide_multiply_fusion.1
  116.6 0.3 reshape.180
  117.3 0.3 divide_multiply_fusion
  118.0 16.2 %while.31 = (s32[]{:T(128)}, f32[2,64,64]{2,1,0:T(8,128)S(1)}, s32[]{:T(128)}, f32[2,256,2,64]{1,0,3,2:T(2,128)S(1)}, s32[2,256]{1,0:T(2,128)S(1)}, /*index=5*/f...) while((s32[]{:T(128)}, f32[2,64,64]{2,1,0:T(8,128)S(1)}, ...), condition=%wide.region_3.4_spmd.clone, body=%wide.region_0.3_spmd.clone.sunk | while | flops 202246672 | bytes 2326889 | solution.py:149
  118.0 0.6 reduce-window.26
  119.2 0.6 dynamic-slice.4
  119.8 0.6 broadcast_compare_fusion.3
  122.0 0.4 fusion.112
  122.6 0.8 fusion.114
  123.6 1.9 dynamic_update_slice.6
  126.1 0.6 reduce-window.26
  127.3 0.6 dynamic-slice.4
  127.9 0.6 broadcast_compare_fusion.3
  130.1 0.4 fusion.112
  130.7 0.8 fusion.114
  131.6 1.9 dynamic_update_slice.6
  134.4 11.6 %all-gather.1 = bf16[16,64,64]{2,1,0:T(8,128)(2,1)S(1)} all-gather(bf16[2,64,64]{2,1,0:T(8,128)(2,1)S(1)} %convert_element_type.85), channel_id=3, replica_groups=mesh['seq'=8,'tensor'=32] {'seq'}, dimensions={0}, use_global_device_ids=true | all-gather | bytes 147456 | tf_op jit(solution)/shard_map/all_gather | solution.py:20
  146.0 6.9 %while.30 = (s32[]{:T(128)}, f32[2,64,64]{2,1,0:T(8,128)S(1)}, f32[1]{0:T(128)}, s32[]{:T(128)}, bf16[8,1]{0,1:T(2,128)(2,1)S(1)}, /*index=5*/bf16[8,2]{0,1:T(2,...) while((s32[]{:T(128)}, f32[2,64,64]{2,1,0:T(8,128)S(1)}, ...), condition=%wide.region_7.8_spmd, body=%wide.region_6.7_spmd.sunk | while | flops 24592 | bytes 82183 | solution.py:36
  146.0 0.6 constant_dynamic-slice_fusion.7
  149.5 0.6 constant_dynamic-slice_fusion.7
  152.9 0.5 fusion.38
  153.6 3.5 multiply_reduce_fusion
  157.1 47.3 %all-gather.5 = f32[32,1,512]{2,1,0:T(1,128)S(1)} all-gather(f32[1,1,512]{2,1,0:T(1,128)S(1)} %bitcast.198), channel_id=5, replica_groups=mesh['seq'=8,'tensor'=32] {'tensor'}, dimensions={0}, use_global_device_ids=true | all-gather | bytes 67584 | tf_op jit(solution)/shard_map/all_gather | solution.py:171
  204.5 3.0 convolution_convert_fusion
  207.5 233.7 %reduce-scatter.2.cloned.1.call-done = bf16[16,3584]{1,0:T(8,128)(2,1)} async-done(((bf16[512,3584]{1,0:T(8,128)(2,1)}), bf16[16,3584]{1,0:T(8,128)(2,1)}) %reduce-scatter.2.cloned.1.call-update) | async-done | bytes 114704 | tf_op jit(solution)/shard_map/reduce_scatter | solution.py:175
  (94 shorter events, 6.5 us)
Async XLA Ops:
  6.5 198.0 %copy-start = (bf16[128,3584]{1,0:T(8,128)(2,1)S(1)}, bf16[128,3584]{1,0:T(8,128)(2,1)}, u32[]{:S(2)}) copy-start(bf16[128,3584]{1,0:T(8,128)(2,1)} %param.26) | copy-start | bytes 2752516
  6.5 86.9 %all-gather.8.cloned.1.call-start = ((), (), s32[]{:S(2)}) async-start(), calls=%async_computation.1 | async-start | bytes 3784704 | tf_op jit(solution)/shard_map/all_gather | solution.py:102
  7.3 433.9 %reduce-scatter.2.cloned.1.call-start = ((), (), s32[]{:S(2)}) async-start(), calls=%async_computation.2 | async-start | bytes 3784704 | tf_op jit(solution)/shard_map/reduce_scatter | solution.py:175
  12.7 19.7 %collective-permute-start = (bf16[3]{0:T(256)(128)(2,1)S(1)}, bf16[3]{0:T(256)(128)(2,1)S(1)}, u32[]{:S(2)}, u32[]{:S(2)}) collective-permute-start(bf16[3]{0:T(256)(128)(2,1)S(1)} %slice.118), channel_id=1, source_target_pairs={{0,32},{32,64},{64,96},{96,128},{128,160},{160,192},{192,224},{1,3... | collective-permute-start | bytes 26 | tf_op jit(solution)/shard_map/ppermute | solution.py:14
  96.1 5.7 %copy-start.2 = (bf16[3584,128]{1,0:T(8,128)(2,1)S(1)}, bf16[3584,128]{1,0:T(8,128)(2,1)}, u32[]{:S(2)}) copy-start(bf16[3584,128]{1,0:T(8,128)(2,1)} %param.18) | copy-start | bytes 2752516
  96.2 5.6 %copy-start.1 = (bf16[512,3584]{0,1:T(8,128)(2,1)S(1)}, bf16[512,3584]{0,1:T(8,128)(2,1)}, u32[]{:S(2)}) copy-start(bf16[512,3584]{0,1:T(8,128)(2,1)} %all-gather.8.cloned.1.call-done) | copy-start | bytes 11010052
  99.9 16.4 %collective-permute-start.1 = (bf16[3,128]{1,0:T(4,128)(2,1)S(1)}, bf16[3,128]{1,0:T(4,128)(2,1)S(1)}, u32[]{:S(2)}, u32[]{:S(2)}) collective-permute-start(bf16[3,128]{1,0:T(4,128)(2,1)S(1)} %slice.152), channel_id=1, source_target_pairs={{0,32},{32,64},{64,96},{96,128},{128,160},{160,192},{192,224},{1,3... | collective-permute-start | bytes 2312 | tf_op jit(solution)/shard_map/ppermute | solution.py:14
  103.0 14.3 %collective-permute-start.2 = (bf16[3,128]{1,0:T(4,128)(2,1)S(1)}, bf16[3,128]{1,0:T(4,128)(2,1)S(1)}, u32[]{:S(2)}, u32[]{:S(2)}) collective-permute-start(bf16[3,128]{1,0:T(4,128)(2,1)S(1)} %slice.157), channel_id=1, source_target_pairs={{0,32},{32,64},{64,96},{96,128},{128,160},{160,192},{192,224},{1,3... | collective-permute-start | bytes 2312 | tf_op jit(solution)/shard_map/ppermute | solution.py:14
  117.9 35.0 %copy-start.3 = (s32[512]{0:T(512)S(1)}, s32[512]{0:T(512)}, u32[]{:S(2)}) copy-start(s32[512]{0:T(512)} %param.27) | copy-start | bytes 6148
  117.9 35.0 %copy-start.5 = (f32[2]{0:T(128)S(1)}, f32[2]{0:T(128)}, u32[]{:S(2)}) copy-start(f32[2]{0:T(128)} %param.22) | copy-start | bytes 28
  153.5 51.1 %copy-start.4 = (f32[128]{0:T(128)S(1)}, f32[128]{0:T(128)}, u32[]{:S(2)}) copy-start(f32[128]{0:T(128)} %param.25) | copy-start | bytes 1540
Sparse Core Ops, SparseCore 0:
  9.9 83.4 all-gather.7
  207.6 233.4 reduce-scatter.1
